TPU v7x, 32 devices: a whole 2x2x4 slice. The times are simulated.
32 devices in a mesh: vocab: 4 (over z), rows: 8 (over y, x, core).
Axes of the slice: x: 2, y: 2, z: 4, core: 2. Of those that a mesh axis runs over, the one named last changes fastest.
Arguments:
- hidden_pass: bfloat16 [96, 64, 4096], P('rows', None, 'vocab'), may hold values from -6 to 6
- hidden_query: bfloat16 [96, 8, 4096], P('rows', None, 'vocab'), may hold values from -6 to 6
- mask_pass: int32 [96, 64], P('rows'), may hold values 0 or 1
- mask_query: int32 [96, 8], P('rows'), may hold values 0 or 1
- labels: int32 [96], P('rows'), may hold values from 0 to 95, each once
- head_weight: bfloat16 [4096, 16384], P('rows', 'vocab'), may hold values from -1 to 1
Outputs:
- grad_pass: bfloat16 [96, 64, 4096], P('rows', None, 'vocab')
- grad_query: bfloat16 [96, 8, 4096], P('rows', None, 'vocab')
Inputs may be any that keep to these rules, and one draw needn't show every extreme that they name: `labels`: each passage is the positive of exactly one query.
All inputs are finite; a program needn't handle non-finite values. No bound on the sum of `mask_pass` or of `mask_query` on one device may be relied on, other than what follows from the above.
Results may differ from a plain program's by a relative error of at most 0.018.
The roundings to bfloat16 on the way count: a program that leaves them out, or rounds other values in their place, can miss the bound.
Values may be sent and summed in bfloat16 or wider, within the bound.
No kernel may reach another device: no remote copies, remote signals or barrier semaphores. Data moves between devices by JAX's collectives and lax.ppermute only.
A program may use at most 128 MiB of HBM per device.

v0:
```python
import jax
import jax.numpy as jnp
from jax import lax
from jax.sharding import PartitionSpec as P

V = 16384
MARGIN = 1.0
SHARPNESS = 16.0


def activate(logits):
    return jnp.log1p(jnp.maximum(logits, 0.0))


def pool_rows(logits, mask, groups, length):
    values = activate(logits).reshape(groups, length, -1)
    weight = mask.astype(jnp.float32)[:, :, None]
    totals = jnp.sum(values**4 * weight, axis=1)
    sparse = (jnp.power(totals + 1.0, 0.25) - 1.0).astype(jnp.bfloat16)
    return (values, totals, sparse)


def logit_slopes(sparse_grad, values, totals, logits, mask, groups, length):
    weight = mask.astype(jnp.float32)[:, :, None]
    factor = sparse_grad * jnp.power(totals + 1.0, -0.75)
    slopes = 1.0 / (1.0 + jnp.maximum(logits, 0.0)).reshape(groups, length, -1)
    gradient = factor[:, None, :] * weight * values**3 * slopes
    return gradient.astype(jnp.bfloat16).reshape(groups * length, -1)


def shards(hidden_pass, hidden_query, mask_pass, mask_query, labels, head_weight):
    groups = hidden_pass.shape[0]
    pass_length = hidden_pass.shape[1]
    query_length = hidden_query.shape[1]
    pass_rows = groups * pass_length
    whole_pass, whole_query = (
        lax.all_gather(hidden_pass, "vocab", axis=2, tiled=True),
        lax.all_gather(hidden_query, "vocab", axis=2, tiled=True),
    )
    tokens = jnp.concatenate(
        [whole_pass.reshape(pass_rows, -1), whole_query.reshape(groups * query_length, -1)], axis=0
    )
    whole_head = lax.all_gather(head_weight, "rows", axis=0, tiled=True)
    logits = jnp.dot(tokens, whole_head, preferred_element_type=jnp.float32)
    logits_pass = logits[:pass_rows]
    logits_query = logits[pass_rows:]
    values_pass, totals_pass, sparse_pass = pool_rows(logits_pass, mask_pass, groups, pass_length)
    values_query, totals_query, sparse_query = pool_rows(
        logits_query, mask_query, groups, query_length
    )
    all_pass = lax.all_gather(sparse_pass, "rows", axis=0, tiled=True)
    partial_scores = lax.dot_general(
        sparse_query, all_pass, (((1,), (1,)), ((), ())), preferred_element_type=jnp.float32
    )
    scaling = SHARPNESS * V ** (-0.5)
    scores = lax.psum(partial_scores, "vocab") * scaling
    onehot = (labels[:, None] == jnp.arange(all_pass.shape[0], dtype=jnp.int32)[None, :]).astype(
        jnp.float32
    )
    positive = jnp.sum(scores * onehot, axis=1, keepdims=True)
    weights = jax.nn.sigmoid(MARGIN + scores - positive) * (1.0 - onehot)
    score_grad = ((weights - onehot * jnp.sum(weights, axis=1, keepdims=True)) * scaling).astype(
        jnp.bfloat16
    )
    query_sparse_grad = jnp.dot(score_grad, all_pass, preferred_element_type=jnp.float32)
    pass_sparse_grad = lax.psum_scatter(
        lax.dot_general(
            score_grad, sparse_query, (((0,), (0,)), ((), ())), preferred_element_type=jnp.float32
        ).astype(jnp.bfloat16),
        "rows",
        scatter_dimension=0,
        tiled=True,
    ).astype(jnp.float32)
    slopes_pass = logit_slopes(
        pass_sparse_grad, values_pass, totals_pass, logits_pass, mask_pass, groups, pass_length
    )
    slopes_query = logit_slopes(
        query_sparse_grad,
        values_query,
        totals_query,
        logits_query,
        mask_query,
        groups,
        query_length,
    )
    slopes = jnp.concatenate([slopes_pass, slopes_query], axis=0)
    partial_terms = lax.dot_general(
        slopes, whole_head, (((1,), (1,)), ((), ())), preferred_element_type=jnp.float32
    )
    summed = lax.psum_scatter(
        partial_terms.astype(jnp.bfloat16), "vocab", scatter_dimension=1, tiled=True
    ).astype(jnp.float32)
    grad_pass = summed[:pass_rows].reshape(groups, pass_length, -1).astype(jnp.bfloat16)
    grad_query = summed[pass_rows:].reshape(groups, query_length, -1).astype(jnp.bfloat16)
    return (grad_pass, grad_query)


def solution(mesh):
    return jax.shard_map(
        shards,
        mesh=mesh,
        in_specs=(
            P("rows", None, "vocab"),
            P("rows", None, "vocab"),
            P("rows", None),
            P("rows", None),
            P("rows"),
            P("rows", "vocab"),
        ),
        out_specs=(P("rows", None, "vocab"), P("rows", None, "vocab")),
        check_vma=False,
    )
```

profile of v0, /device:TPU:0, one launch (start us, length us, event | category | flops | bytes accessed | tf_op | source)
XLA Modules:
  0.0 589.9 jit_solution(8366883273311622980)
XLA Ops:
  7.2 0.7 all-gather.4.cloned.1.call-update
  7.9 0.7 all-gather.6.cloned.1.call-update
  8.7 0.7 convert_element_type.48
  9.4 0.7 convert_element_type.46
  10.3 1.2 dynamic-slice.4
  12.2 29.5 %all_gather.13 = bf16[12,8,4096]{2,1,0:T(8,128)(2,1)S(1)} all-gather(bf16[12,8,1024]{2,1,0:T(8,128)(2,1)} %param.7), channel_id=1, replica_groups=mesh['vocab'=4,'rows'=8] {'vocab'}, dimensions={2}, use_global_device_ids=true | all-gather | bytes 983040 | tf_op jit(solution)/shard_map/all_gather | solution.py:38
  41.7 91.9 %all-gather.4.cloned.1.call-done = bf16[12,64,4096]{2,1,0:T(8,128)(2,1)} async-done(((bf16[12,64,1024]{2,1,0:T(8,128)(2,1)}), bf16[12,64,4096]{2,1,0:T(8,128)(2,1)}) %all-gather.4.cloned.1.call-update) | async-done | bytes 6291472 | tf_op jit(solution)/shard_map/all_gather | solution.py:37
  133.5 162.8 %all-gather.6.cloned.1.call-done = bf16[4096,4096]{1,0:T(8,128)(2,1)} async-done(((bf16[512,4096]{1,0:T(8,128)(2,1)}), bf16[4096,4096]{1,0:T(8,128)(2,1)}) %all-gather.6.cloned.1.call-update) | async-done | bytes 33554448 | tf_op jit(solution)/shard_map/all_gather | solution.py:43
  296.3 36.8 %fusion.4 = f32[864,4096]{1,0:T(8,128)} fusion(bf16[4096,4096]{1,0:T(8,128)(2,1)} %all-gather.6.cloned.1.call-done, bf16[96,4096]{1,0:T(8,128)(2,1)S(1)} %bitcast.31, bf16[768,4096]{1,0:T(8,128)(2,1)} %bitcast.32), kind=kOutput, calls=%fused_computation.8 | convolution fusion | flops 29005185024 | bytes 54788096 | tf_op jit(solution)/shard_map/dot_general | solution.py:44
  333.1 14.0 %multiply_multiply_fusion.1 = f32[768,4096]{1,0:T(8,128)} fusion(f32[864,4096]{1,0:T(8,128)} %fusion.4), kind=kLoop, calls=%fused_computation.1 | loop fusion | flops 9437184 | bytes 25165824 | tf_op jit(solution)/shard_map/mul | solution.py:18
  347.1 2.4 fusion.17
  349.6 6.6 %multiply_reduce_fusion = f32[12,4096]{1,0:T(8,128)S(1)} fusion(f32[12,64,4096]{2,1,0:T(8,128)} %bitcast.29, f32[12,64]{1,0:T(8,128)S(1)} %convert_element_type.48), kind=kLoop, calls=%fused_computation.7 | loop fusion | flops 6242304 | bytes 12782592 | tf_op jit(solution)/shard_map/reduce_sum | solution.py:18
  356.3 10.9 %all-gather = bf16[8,12,4096]{2,1,0:T(8,128)(2,1)S(1)} all-gather(bf16[1,12,4096]{2,1,0:T(8,128)(2,1)S(1)} %fusion.21), channel_id=1, replica_groups=mesh['vocab'=4,'rows'=8] {'rows'}, dimensions={0}, use_global_device_ids=true | all-gather | bytes 884736 | tf_op jit(solution)/shard_map/all_gather | solution.py:51
  367.2 0.2 reshape.38
  367.4 0.3 fusion.22
  367.7 11.8 %psum.7 = f32[12,96]{1,0:T(8,128)S(1)} all-reduce(f32[12,96]{1,0:T(8,128)S(1)} %fusion.22), channel_id=1, replica_groups=mesh['vocab'=4,'rows'=8] {'vocab'}, use_global_device_ids=true, to_apply=%region_2.0 | all-reduce | flops 1152 | bytes 9216 | tf_op jit(solution)/shard_map/psum | solution.py:56
  379.5 0.2 select_reduce_fusion
  379.7 0.2 fusion.31
  379.9 0.5 convolution_convert_fusion
  380.4 18.0 %fusion = bf16[16,4096]{1,0:T(8,128)(2,1)S(1)} fusion(bf16[96,4096]{1,0:T(8,128)(2,1)S(1)} %convolution_convert_fusion), kind=kCustom, calls=%all-reduce-scatter | all-reduce-scatter fusion | flops 524289 | bytes 918016
  398.5 1.3 collective-permute-start
  399.8 0.3 convolution_multiply_fusion
  400.1 3.0 collective-permute-start.1
  403.1 2.3 fusion.20
  405.4 0.2 collective-permute-done.1
  405.6 0.8 concatenate.8
  406.5 0.2 power_multiply_fusion
  406.6 11.0 %fusion.3 = bf16[768,4096]{1,0:T(8,128)(2,1)} fusion(f32[864,4096]{1,0:T(8,128)} %fusion.4, f32[768]{0:T(1024)S(1)} %mul.135, f32[12,4096]{1,0:T(8,128)S(1)} %power_multiply_fusion), kind=kLoop, calls=%fused_computation.4 | loop fusion | flops 28311552 | bytes 19074048 | tf_op jit(solution)/shard_map/convert_element_type | solution.py:28
  417.7 36.4 %fusion.12 = bf16[864,4096]{1,0:T(8,128)(2,1)} fusion(bf16[4096,4096]{1,0:T(8,128)(2,1)} %all-gather.6.cloned.1.call-done, bf16[96,4096]{1,0:T(8,128)(2,1)S(1)} %fusion.20, bf16[768,4096]{1,0:T(8,128)(2,1)} %fusion.3), kind=kOutput, calls=%fused_computation.16 | convolution fusion | flops 29008723968 | bytes 47710208 | tf_op jit(solution)/shard_map/dot_general | solution.py:87
  454.1 125.0 %reduce-scatter.4.cloned.1.call-done = bf16[864,1024]{1,0:T(8,128)(2,1)} async-done(((bf16[864,4096]{1,0:T(8,128)(2,1)}), bf16[864,1024]{1,0:T(8,128)(2,1)}) %reduce-scatter.4.cloned.1.call-update) | async-done | bytes 1769488 | tf_op jit(solution)/shard_map/reduce_scatter | solution.py:90
  579.1 2.7 slice.20
  581.7 1.6 slice_bitcast_fusion
  (12 shorter events, 0.5 us)
Async XLA Ops:
  7.2 126.4 %all-gather.4.cloned.1.call-start = ((), (), s32[]{:S(2)}) async-start(), calls=%async_computation.1 | async-start | bytes 7864320 | tf_op jit(solution)/shard_map/all_gather | solution.py:37
  7.9 288.4 %all-gather.6.cloned.1.call-start = ((), (), s32[]{:S(2)}) async-start(), calls=%async_computation.2 | async-start | bytes 37748736 | tf_op jit(solution)/shard_map/all_gather | solution.py:43
  8.6 570.4 %reduce-scatter.4.cloned.1.call-start = ((), (), s32[]{:S(2)}) async-start(), calls=%async_computation.3 | async-start | bytes 8847360 | tf_op jit(solution)/shard_map/reduce_scatter | solution.py:90
  349.5 30.0 %copy-start = (s32[12]{0:T(128)S(1)}, s32[12]{0:T(128)}, u32[]{:S(2)}) copy-start(s32[12]{0:T(128)} %param.10) | copy-start | bytes 148
  398.5 7.1 %collective-permute-start = (bf16[16,4096]{1,0:T(8,128)(2,1)S(1)}, bf16[16,4096]{1,0:T(8,128)(2,1)S(1)}, u32[]{:S(2)}, u32[]{:S(2)}) collective-permute-start(bf16[16,4096]{1,0:T(8,128)(2,1)S(1)} %fusion), channel_id=1, source_target_pairs={{0,1},{1,2},{2,3},{3,4},{4,5},{5,6},{6,7},{8,9},{9,10},{10,11},{11... | collective-permute-start | bytes 393224
  400.1 5.5 collective-permute-start.1
Sparse Core Ops, SparseCore 0:
  9.5 123.9 all-gather.3
  135.4 160.8 all-gather.5
  454.2 124.8 reduce-scatter.3
where the time goes:
time: 590 us
  waiting for transfers between devices  381 us (65%)
  matrix products  74.3 us (13%)
  blocking collectives  70.2 us (12%)
  other arithmetic  38.4 us (7%)
  between operations  14.5 us (2%)
  local copies, waits for them, and re-layouts  6.81 us (1%)
    all_gather x1, waiting for transfers between devices, shards(): whole_head = lax.all_gather(head_weight, 'rows', axis=0, tiled=True)  163 us
    reduce_scatter x1, waiting for transfers between devices, shards(): lax.psum_scatter(partial_terms.astype(jnp.bfloat16), 'vocab', scatter_dim...  125 us
    all_gather x1, waiting for transfers between devices, shards(): lax.all_gather(hidden_pass, 'vocab', axis=2, tiled=True)  91.9 us
    dot_general x1, matrix products, shards(): logits = jnp.dot(tokens, whole_head, preferred_element_type=jnp.float32)  36.8 us
    dot_general x1, matrix products, shards(): lax.dot_general(slopes, whole_head, (((1,), (1,)), ((), ())), preferred_e...  36.4 us
    all_gather x1, blocking collectives, shards(): lax.all_gather(hidden_query, 'vocab', axis=2, tiled=True)  29.5 us
    unnamed x1, blocking collectives  18 us
    mul x1, other arithmetic, pool_rows(): totals = jnp.sum(values ** 4 * weight, axis=1)  14 us
  transfers between devices with their start and end apart: 5, of which 4 were waited for; matrix products, arithmetic and copies ran while one was open for 1% of the time, Pallas kernels for 0%

commit v1 on v0

--- a/solution.py
+++ b/solution.py
@@ -6,6 +6,28 @@
 V = 16384
 MARGIN = 1.0
 SHARPNESS = 16.0
+
+
+def joined_along(tiles, dim):
+    tiles = jnp.moveaxis(tiles, 0, dim)
+    dims = tiles.shape
+    return tiles.reshape(*dims[:dim], dims[dim] * dims[dim + 1], *dims[dim + 2 :])
+
+
+def doubled(value, axis):
+    devices = lax.axis_size(axis)
+    tiles = value[None]
+    for level in range(devices.bit_length() - 1):
+        stride = 1 << level
+        received = lax.ppermute(tiles, axis, [(i, i ^ stride) for i in range(devices)])
+        both = jnp.stack([tiles, received])
+        upper = lax.axis_index(axis) >> level & 1
+        tiles = jnp.where(upper == 0, both, both[::-1]).reshape(-1, *value.shape)
+    return tiles
+
+
+def doubled_up(x, axis, dim):
+    return joined_along(doubled(x, axis), dim)
 
 
 def activate(logits):
@@ -34,7 +56,7 @@
     query_length = hidden_query.shape[1]
     pass_rows = groups * pass_length
     whole_pass, whole_query = (
-        lax.all_gather(hidden_pass, "vocab", axis=2, tiled=True),
+        doubled_up(hidden_pass, "vocab", 2),
         lax.all_gather(hidden_query, "vocab", axis=2, tiled=True),
     )
     tokens = jnp.concatenate(

time: 590 us -> 540 us (0.915); the launches traced: 590 us -> 530 us
  waiting for transfers between devices: 381 us -> 173 us
  blocking collectives: 70.2 us -> 189 us
  local copies, waits for them, and re-layouts: 6.81 us -> 23.2 us
  other arithmetic: 38.4 us -> 46.1 us
    all_gather x1, waiting for transfers between devices: 163 us -> 11.5 us  [shards(): whole_head = lax.all_gather(head_weight, 'rows', axis=0, tiled=True)]
    all_gather x1, blocking collectives: 29.5 us -> 150 us  [shards(): lax.all_gather(hidden_query, 'vocab', axis=2, tiled=True)]
    all_gather x1 -> x0, waiting for transfers between devices: 91.9 us -> none  [shards(): lax.all_gather(hidden_pass, 'vocab', axis=2, tiled=True)]
    ppermute x0 -> x2, waiting for transfers between devices: none -> 34.6 us  [doubled(): lax.ppermute(tiles, axis, [(i, i ^ stride) for i in range(devices)])]
    unnamed x6 -> x17, local copies, waits for them, and re-layouts: 2.29 us -> 11.2 us
    reshape x0 -> x1, local copies, waits for them, and re-layouts: none -> 7.49 us  [doubled(): tiles = jnp.where(upper == 0, both, both[::-1]).reshape(-1, *value.shape)]
    another operation x0 -> x3, other arithmetic: none -> 7.02 us  [doubled(): both = jnp.stack([tiles, received])]
  transfers between devices with their start and end apart: 5 -> 6, of which waited for: 4 -> 4; matrix products, arithmetic and copies ran while one was open for 1% -> 6% of each run, Pallas kernels for 0% -> 0%
where the time goes in v1:
time: 540 us; the launch traced here: 530 us
  blocking collectives  189 us (35%)
  waiting for transfers between devices  173 us (32%)
  matrix products  74.3 us (14%)
  other arithmetic  46.1 us (9%)
  local copies, waits for them, and re-layouts  23.2 us (4%)
  between operations  15.3 us (3%)
  starting transfers between devices  8.66 us (2%)
    all_gather x1, blocking collectives, shards(): lax.all_gather(hidden_query, 'vocab', axis=2, tiled=True)  150 us
    reduce_scatter x1, waiting for transfers between devices, shards(): lax.psum_scatter(partial_terms.astype(jnp.bfloat16), 'vocab', scatter_dim...  126 us
    dot_general x1, matrix products, shards(): logits = jnp.dot(tokens, whole_head, preferred_element_type=jnp.float32)  36.8 us
    dot_general x1, matrix products, shards(): lax.dot_general(slopes, whole_head, (((1,), (1,)), ((), ())), preferred_e...  36.4 us
    ppermute x2, waiting for transfers between devices, doubled(): lax.ppermute(tiles, axis, [(i, i ^ stride) for i in range(devices)])  34.6 us
    unnamed x1, blocking collectives  19.4 us
    mul x1, other arithmetic, pool_rows(): totals = jnp.sum(values ** 4 * weight, axis=1)  14 us
    convert_element_type x2, other arithmetic, logit_slopes(): return gradient.astype(jnp.bfloat16).reshape(groups * length, -1)  13.3 us
  transfers between devices with their start and end apart: 6, of which 4 were waited for; matrix products, arithmetic and copies ran while one was open for 6% of the time, Pallas kernels for 0%

profile of v1, /device:TPU:0, one launch (start us, length us, event | category | flops | bytes accessed | tf_op | source)
XLA Modules:
  0.0 529.8 jit_solution(3018798428975567268)
XLA Ops:
  7.2 0.7 all-gather.3.cloned.1.call-update
  7.9 3.1 collective-permute-start
  11.1 34.6 %collective-permute-done = bf16[1,12,64,1024]{3,2,1,0:T(8,128)(2,1)S(1)} collective-permute-done((bf16[1,12,64,1024]{3,2,1,0:T(8,128)(2,1)}, bf16[1,12,64,1024]{3,2,1,0:T(8,128)(2,1)S(1)}, u32[]{:S(2)}, u32[]{:S(2)}) %collective-permute-start) | collective-permute-done | bytes 1572896 | tf_op jit(solution)/shard_map/ppermute | solution.py:22
  45.7 1.7 pad_maximum_fusion.1
  47.4 2.9 fusion.16
  50.3 2.8 collective-permute-start.1
  53.3 0.6 dynamic-slice.4
  54.5 149.9 %all_gather.9 = bf16[12,8,4096]{2,1,0:T(8,128)(2,1)} all-gather(bf16[12,8,1024]{2,1,0:T(8,128)(2,1)S(1)} %copy-done.1), channel_id=1, replica_groups=mesh['vocab'=4,'rows'=8] {'vocab'}, dimensions={2}, use_global_device_ids=true | all-gather | bytes 983040 | tf_op jit(solution)/shard_map/all_gather | solution.py:60
  204.5 2.5 pad_maximum_fusion
  207.0 2.1 reverse_select_fusion
  209.1 7.5 %copy.13 = bf16[4,12,64,1024]{3,0,2,1:T(4,128)(2,1)} copy(bf16[4,12,64,1024]{3,2,1,0:T(8,128)(2,1)S(1)} %bitcast.42) | data formatting | bytes 12582912 | tf_op jit(solution)/shard_map/reshape | solution.py:25
  216.6 9.5 %copy.16 = bf16[96,8,4,1024]{3,1,2,0:T(8,128)(2,1)} copy(bf16[96,8,4,1024]{3,2,1,0:T(4,128)(2,1)} %bitcast.43) | data formatting | bytes 12582912
  226.1 11.5 %all-gather.3.cloned.1.call-done = bf16[4096,4096]{1,0:T(8,128)(2,1)} async-done(((bf16[512,4096]{1,0:T(8,128)(2,1)}), bf16[4096,4096]{1,0:T(8,128)(2,1)}) %all-gather.3.cloned.1.call-update) | async-done | bytes 33554448 | tf_op jit(solution)/shard_map/all_gather | solution.py:65
  237.7 36.8 %fusion.4 = f32[864,4096]{1,0:T(8,128)} fusion(bf16[4096,4096]{1,0:T(8,128)(2,1)} %all-gather.3.cloned.1.call-done, bf16[96,4096]{1,0:T(8,128)(2,1)S(1)} %bitcast.49, bf16[768,4096]{1,0:T(8,128)(2,1)} %bitcast.44), kind=kOutput, calls=%fused_computation.9 | convolution fusion | flops 29005185024 | bytes 54788096 | tf_op jit(solution)/shard_map/dot_general | solution.py:66
  274.4 14.0 %multiply_multiply_fusion.1 = f32[768,4096]{1,0:T(8,128)} fusion(f32[864,4096]{1,0:T(8,128)} %fusion.4), kind=kLoop, calls=%fused_computation.1 | loop fusion | flops 9437184 | bytes 25165824 | tf_op jit(solution)/shard_map/mul | solution.py:40
  288.4 2.4 fusion.19
  290.9 6.6 %multiply_reduce_fusion = f32[12,4096]{1,0:T(8,128)S(1)} fusion(f32[12,64,4096]{2,1,0:T(8,128)} %bitcast.41, f32[12,64]{1,0:T(8,128)S(1)} %convert_element_type.48), kind=kLoop, calls=%fused_computation.7 | loop fusion | flops 6242304 | bytes 12782592 | tf_op jit(solution)/shard_map/reduce_sum | solution.py:40
  297.6 10.9 %all-gather = bf16[8,12,4096]{2,1,0:T(8,128)(2,1)S(1)} all-gather(bf16[1,12,4096]{2,1,0:T(8,128)(2,1)S(1)} %fusion.23), channel_id=1, replica_groups=mesh['vocab'=4,'rows'=8] {'rows'}, dimensions={0}, use_global_device_ids=true | all-gather | bytes 884736 | tf_op jit(solution)/shard_map/all_gather | solution.py:73
  308.7 0.3 fusion.24
  309.0 8.8 %psum.7 = f32[12,96]{1,0:T(8,128)S(1)} all-reduce(f32[12,96]{1,0:T(8,128)S(1)} %fusion.24), channel_id=1, replica_groups=mesh['vocab'=4,'rows'=8] {'vocab'}, use_global_device_ids=true, to_apply=%region_2.3 | all-reduce | flops 1152 | bytes 9216 | tf_op jit(solution)/shard_map/psum | solution.py:78
  318.2 0.5 convolution_convert_fusion
  318.7 19.4 %fusion = bf16[16,4096]{1,0:T(8,128)(2,1)S(1)} fusion(bf16[96,4096]{1,0:T(8,128)(2,1)S(1)} %convolution_convert_fusion), kind=kCustom, calls=%all-reduce-scatter | all-reduce-scatter fusion | flops 524289 | bytes 918016
  338.2 1.3 collective-permute-start.2
  339.5 0.3 convolution_multiply_fusion
  339.8 1.4 collective-permute-start.3
  341.2 2.3 fusion.22
  343.7 0.8 concatenate.8
  344.7 11.0 %fusion.3 = bf16[768,4096]{1,0:T(8,128)(2,1)} fusion(f32[864,4096]{1,0:T(8,128)} %fusion.4, f32[768]{0:T(1024)S(1)} %mul.135, f32[12,4096]{1,0:T(8,128)S(1)} %power_multiply_fusion), kind=kLoop, calls=%fused_computation.4 | loop fusion | flops 28311552 | bytes 19074048 | tf_op jit(solution)/shard_map/convert_element_type | solution.py:50
  355.7 36.4 %fusion.12 = bf16[864,4096]{1,0:T(8,128)(2,1)} fusion(bf16[4096,4096]{1,0:T(8,128)(2,1)} %all-gather.3.cloned.1.call-done, bf16[96,4096]{1,0:T(8,128)(2,1)S(1)} %fusion.22, bf16[768,4096]{1,0:T(8,128)(2,1)} %fusion.3), kind=kOutput, calls=%fused_computation.17 | convolution fusion | flops 29008723968 | bytes 47710208 | tf_op jit(solution)/shard_map/dot_general | solution.py:109
  392.1 126.2 %reduce-scatter.4.cloned.1.call-done = bf16[864,1024]{1,0:T(8,128)(2,1)} async-done(((bf16[864,4096]{1,0:T(8,128)(2,1)}), bf16[864,1024]{1,0:T(8,128)(2,1)}) %reduce-scatter.4.cloned.1.call-update) | async-done | bytes 1769488 | tf_op jit(solution)/shard_map/reduce_scatter | solution.py:112
  518.3 2.7 slice.20
  521.0 1.6 slice_bitcast_fusion
  (29 shorter events, 1.5 us)
Async XLA Ops:
  7.2 230.5 %all-gather.3.cloned.1.call-start = ((), (), s32[]{:S(2)}) async-start(), calls=%async_computation.1 | async-start | bytes 37748736 | tf_op jit(solution)/shard_map/all_gather | solution.py:65
  7.9 510.4 %reduce-scatter.4.cloned.1.call-start = ((), (), s32[]{:S(2)}) async-start(), calls=%async_computation.2 | async-start | bytes 8847360 | tf_op jit(solution)/shard_map/reduce_scatter | solution.py:112
  7.9 37.7 %collective-permute-start = (bf16[1,12,64,1024]{3,2,1,0:T(8,128)(2,1)}, bf16[1,12,64,1024]{3,2,1,0:T(8,128)(2,1)S(1)}, u32[]{:S(2)}, u32[]{:S(2)}) collective-permute-start(bf16[1,12,64,1024]{3,2,1,0:T(8,128)(2,1)} %bitcast.46), channel_id=1, source_target_pairs={{0,8},{8,0},{16,24},{24,16},{1,9},{9,1},{17,25},{25,17},{2,10},{10... | collective-permute-start | bytes 4718600 | tf_op jit(solution)/shard_map/ppermute | solution.py:22
  47.4 5.7 %copy-start.3 = (s32[12,64]{1,0:T(8,128)S(1)}, s32[12,64]{1,0:T(8,128)}, u32[]{:S(2)}) copy-start(s32[12,64]{1,0:T(8,128)} %param.8) | copy-start | bytes 9220
  47.4 5.7 %copy-start.4 = (s32[12,8]{0,1:T(8,128)S(1)}, s32[12,8]{0,1:T(8,128)}, u32[]{:S(2)}) copy-start(s32[12,8]{0,1:T(8,128)} %param.9) | copy-start | bytes 1156
  47.4 5.9 %copy-start.5 = (u32[32]{0:T(128)S(1)}, u32[32]{0:T(128)}, u32[]{:S(2)}) copy-start(u32[32]{0:T(128)} %constant.38) | copy-start | bytes 388
  47.4 7.1 %copy-start.1 = (bf16[12,8,1024]{2,1,0:T(8,128)(2,1)S(1)}, bf16[12,8,1024]{2,1,0:T(8,128)(2,1)}, u32[]{:S(2)}) copy-start(bf16[12,8,1024]{2,1,0:T(8,128)(2,1)} %param.7) | copy-start | bytes 589828
  50.3 154.2 %collective-permute-start.1 = (bf16[2,12,64,1024]{3,2,1,0:T(8,128)(2,1)}, bf16[2,12,64,1024]{3,2,1,0:T(8,128)(2,1)}, u32[]{:S(2)}, u32[]{:S(2)}) collective-permute-start(bf16[2,12,64,1024]{3,2,1,0:T(8,128)(2,1)} %get-tuple-element.3), channel_id=1, source_target_pairs={{0,16},{8,24},{16,0},{24,8},{1,17},{9,25},{17,1},{25,9},{2,18},{10... | collective-permute-start | bytes 9437192 | tf_op jit(solution)/shard_map/ppermute | solution.py:22
  216.6 21.1 %copy-start = (bf16[12,8,4096]{2,1,0:T(8,128)(2,1)S(1)}, bf16[12,8,4096]{2,1,0:T(8,128)(2,1)}, u32[]{:S(2)}) copy-start(bf16[12,8,4096]{2,1,0:T(8,128)(2,1)} %all_gather.9) | copy-start | bytes 2359300
  290.9 26.9 %copy-start.2 = (s32[12]{0:T(128)S(1)}, s32[12]{0:T(128)}, u32[]{:S(2)}) copy-start(s32[12]{0:T(128)} %param.10) | copy-start | bytes 148
  338.2 5.5 %collective-permute-start.2 = (bf16[16,4096]{1,0:T(8,128)(2,1)S(1)}, bf16[16,4096]{1,0:T(8,128)(2,1)S(1)}, u32[]{:S(2)}, u32[]{:S(2)}) collective-permute-start(bf16[16,4096]{1,0:T(8,128)(2,1)S(1)} %fusion), channel_id=1, source_target_pairs={{0,1},{1,2},{2,3},{3,4},{4,5},{5,6},{6,7},{8,9},{9,10},{10,11},{11... | collective-permute-start | bytes 393224
  339.8 3.9 collective-permute-start.3
Sparse Core Ops, SparseCore 0:
  9.9 163.3 all-gather.2
  392.2 126.0 reduce-scatter.3
